TPU v7x, 32 devices: a whole 2x2x4 slice. The times are simulated.
32 devices in a mesh: grp: 2 (over x), gx: 16 (over z, y, core).
Axes of the slice: x: 2, y: 2, z: 4, core: 2. Of those that a mesh axis runs over, the one named last changes fastest.
Arguments:
- grain_ids: int32 [96, 32, 512], P(('grp', 'gx')), parts along dimension 0, may hold values from 0 to 7
- jitter: bfloat16 [8, 96, 32, 512], P(None, ('grp', 'gx')), parts along dimension 1, may hold values from 0 to 0.5
- class_table: int32 [8, 8], replicated, may hold values from 0 to 3
- chosen: int32 [2], replicated, may hold values from 0 to 7
Outputs:
- order_params: float32 [8, 96, 32, 512], P(None, ('grp', 'gx')), parts along dimension 1
- correlation: float32 [2, 96, 32, 512], P(None, ('grp', 'gx')), parts along dimension 1
There are 2 independent parts, one for each index of `grp`. A program takes and returns all parts, laid end to end along the dimension named above; an argument that names none is the same for every part. Nothing has to cross between parts.
All inputs are finite; a program needn't handle non-finite values.
Results may differ from a plain program's by a relative error of at most 0.0003.
Values sent between devices are 32-bit elements; how exact they have to be, the bound alone decides.
No kernel may reach another device: no remote copies, remote signals or barrier semaphores. Data moves between devices by JAX's collectives and lax.ppermute only.
A program may use at most 128 MiB of HBM per device.

v0:
```python
import math
import jax
import jax.numpy as jnp
from jax import lax
from jax.sharding import PartitionSpec as P

STEPS = 3
HIGH = lax.Precision.HIGHEST


def with_halo(value, sides, width):
    for axis, dim in sides:
        peers, length = (lax.axis_size(axis), value.shape[dim])
        up = [(i, (i + 1) % peers) for i in range(peers)]
        down = [(j, i) for i, j in up]
        last = lax.slice_in_dim(value, length - width, length, axis=dim)
        initial = lax.slice_in_dim(value, 0, width, axis=dim)
        before = lax.ppermute(last, axis, up)
        after = lax.ppermute(initial, axis, down)
        value = jnp.concatenate([before, value, after], axis=dim)
    return value


def tables(length):
    index = lax.iota(jnp.int32, length)
    product = index[:, None] * index[None, :] % length
    angle = product.astype(jnp.float32) * (2.0 * math.pi / length)
    return (jnp.cos(angle), jnp.sin(angle))


def onehot_of(grain_ids):
    return (grain_ids[None] == lax.iota(jnp.int32, 8)[:, None, None, None]).astype(jnp.float32)


def levels_map(onehot, class_table):
    levels = 0.4 + 0.2 * class_table.astype(jnp.float32)
    return jnp.einsum("gi,gxzy->ixzy", levels, onehot, precision=HIGH)


def advance(extended, mobility):
    center = extended[:, 1:-1]
    lap = extended[:, 2:] + extended[:, :-2]
    lap = lap + jnp.roll(center, -1, 2) + jnp.roll(center, 1, 2)
    lap = lap + jnp.roll(center, -1, 3) + jnp.roll(center, 1, 3)
    lap = lap - 6.0 * center
    total = jnp.sum(center * center, axis=0)
    drive = -center + center * center * center + 3.0 * center * (total[None] - center * center)
    return center - 0.12 * mobility * (drive - lap)


def forward_planes(fields, cos_y, sin_y, cos_z, sin_z):
    real_y = jnp.dot(fields, cos_y, precision=HIGH)
    imag_y = -jnp.dot(fields, sin_y, precision=HIGH)
    real_z = jnp.einsum("kz,fxzy->fxky", cos_z, real_y, precision=HIGH) + jnp.einsum(
        "kz,fxzy->fxky", sin_z, imag_y, precision=HIGH
    )
    imag_z = jnp.einsum("kz,fxzy->fxky", cos_z, imag_y, precision=HIGH) - jnp.einsum(
        "kz,fxzy->fxky", sin_z, real_y, precision=HIGH
    )
    planes = fields.shape[1]
    return (
        real_z.reshape(fields.shape[0], planes, -1),
        imag_z.reshape(fields.shape[0], planes, -1),
    )


def line_power(real_part, imag_part, cos_x, sin_x, offset):
    real_x = jnp.einsum("kx,fxc->fkc", cos_x, real_part, precision=HIGH) + jnp.einsum(
        "kx,fxc->fkc", sin_x, imag_part, precision=HIGH
    )
    imag_x = jnp.einsum("kx,fxc->fkc", cos_x, imag_part, precision=HIGH) - jnp.einsum(
        "kx,fxc->fkc", sin_x, real_part, precision=HIGH
    )
    power = real_x * real_x + imag_x * imag_x
    freq_x = lax.iota(jnp.int32, power.shape[1])[:, None]
    column = offset + lax.iota(jnp.int32, power.shape[2])[None, :]
    keep = jnp.logical_not(jnp.logical_and(freq_x == 0, column == 0))
    power = power * keep.astype(jnp.float32)[None]
    back_real = jnp.einsum("kx,fkc->fxc", cos_x, power, precision=HIGH)
    back_imag = jnp.einsum("kx,fkc->fxc", sin_x, power, precision=HIGH)
    return (back_real, back_imag)


def inverse_planes(back_real, back_imag, cos_y, sin_y, cos_z, sin_z, depth, width, count):
    fields = back_real.shape[0]
    planes = back_real.shape[1]
    back_real = back_real.reshape(fields, planes, depth, width)
    back_imag = back_imag.reshape(fields, planes, depth, width)
    real_z = jnp.einsum("kz,fxky->fxzy", cos_z, back_real, precision=HIGH) - jnp.einsum(
        "kz,fxky->fxzy", sin_z, back_imag, precision=HIGH
    )
    imag_z = jnp.einsum("kz,fxky->fxzy", cos_z, back_imag, precision=HIGH) + jnp.einsum(
        "kz,fxky->fxzy", sin_z, back_real, precision=HIGH
    )
    result = jnp.dot(real_z, cos_y, precision=HIGH) - jnp.dot(imag_z, sin_y, precision=HIGH)
    return result / (count * count)


def shards(grain_ids, jitter, class_table, chosen):
    planes = grain_ids.shape[0]
    depth = grain_ids.shape[1]
    width = grain_ids.shape[2]
    devices = lax.axis_size("gx")
    onehot = onehot_of(grain_ids)
    eta = 0.6 * onehot + jitter.astype(jnp.float32)
    mobility = levels_map(onehot, class_table)
    for step in range(STEPS):
        extended = with_halo(eta, (("gx", 1),), 1)
        eta = advance(extended, mobility)
    select = (chosen[:, None] == lax.iota(jnp.int32, 8)[None, :]).astype(jnp.float32)
    fields = jnp.einsum("ki,ixzy->kxzy", select, eta, precision=HIGH)
    cos_y, sin_y = tables(width)
    cos_z, sin_z = tables(depth)
    total_x = planes * devices
    cos_x, sin_x = tables(total_x)
    count = float(total_x * depth * width)
    columns = depth * width // devices
    offset = lax.axis_index("gx") * columns
    real_part, imag_part = forward_planes(fields, cos_y, sin_y, cos_z, sin_z)
    stacked = jnp.concatenate([real_part, imag_part], axis=0)
    lines = lax.all_to_all(stacked, "gx", split_axis=2, concat_axis=1, tiled=True)
    back_real, back_imag = line_power(lines[:2], lines[2:], cos_x, sin_x, offset)
    returned = lax.all_to_all(
        jnp.concatenate([back_real, back_imag], axis=0),
        "gx",
        split_axis=1,
        concat_axis=2,
        tiled=True,
    )
    correlation = inverse_planes(
        returned[:2], returned[2:], cos_y, sin_y, cos_z, sin_z, depth, width, count
    )
    return (eta, correlation)


def solution(mesh):
    in_specs = (P(("grp", "gx"), None, None), P(None, ("grp", "gx"), None, None), P(), P())
    out_specs = (P(None, ("grp", "gx"), None, None), P(None, ("grp", "gx"), None, None))
    return jax.shard_map(shards, mesh=mesh, in_specs=in_specs, out_specs=out_specs, check_vma=False)
```

profile of v0, /device:TPU:11, one launch (start us, length us, event | category | flops | bytes accessed | tf_op | source)
XLA Modules:
  0.0 307.3 jit_solution(3220175203014402098)
XLA Ops:
  0.6 1.8 convert_add_fusion
  2.5 0.7 collective-permute-start
  3.3 1.2 collective-permute-start.1
  5.1 14.7 %multiply_subtract_fusion.2 = f32[8,3,32,512]{3,0,2,1:T(8,128)S(1)} fusion(bf16[8,3,32,512]{3,2,1,0:T(8,128)(2,1)S(1)} %copy-done.1, s32[3,32,512]{2,1,0:T(8,128)S(1)} %copy-done), kind=kOutput, calls=%fused_computation.12 | output fusion | flops 4374535 | bytes 2555904 | tf_op jit(solution)/shard_map/sub | solution.py:47
  20.6 2.2 fusion.16
  23.7 1.6 collective-permute-start.3
  25.9 11.9 %collective-permute-done.2 = f32[8,1,32,512]{3,0,2,1:T(8,128)S(1)} collective-permute-done((f32[8,1,32,512]{3,0,2,1:T(8,128)S(1)}, f32[8,1,32,512]{3,0,2,1:T(8,128)S(1)}, u32[]{:S(2)}, u32[]{:S(2)}) %collective-permute-start.2) | collective-permute-done | bytes 524320 | tf_op jit(solution)/shard_map/ppermute | solution.py:19
  37.8 34.6 %fusion.21 = f32[8,3,32,512]{3,0,2,1:T(8,128)S(1)} fusion(f32[8,3,32,512]{3,0,2,1:T(8,128)S(1)} %get-tuple-element.42, f32[8,3,32,512]{3,0,2,1:T(8,128)S(1)} %get-tuple-element.43, f32[8,1,32,512]{3,0,2,1:T(8,128)S(1)} %collective-permute-done.3, f32[8,1,32,512]{3,0,2,1:T(8,128)S(1)} %collective-permute-done.2, f32[8,3,1,512]{3,0,2,1:T(8,128)S(1)} %get-tuple-element.23, ...), kind=kOutput, calls=%fused_computation.24 | output fusion | flops 9879559 | bytes 12058624 | tf_op jit(solution)/shard_map/sub | solution.py:47
  73.2 2.3 collective-permute-start.5
  76.0 11.4 %collective-permute-done.4 = f32[8,1,32,512]{3,0,2,1:T(8,128)S(1)} collective-permute-done((f32[8,1,32,512]{3,0,2,1:T(8,128)S(1)}, f32[8,1,32,512]{3,0,2,1:T(8,128)S(1)}, u32[]{:S(2)}, u32[]{:S(2)}) %collective-permute-start.4) | collective-permute-done | bytes 524320 | tf_op jit(solution)/shard_map/ppermute | solution.py:19
  87.4 34.6 %fusion.26 = f32[8,3,32,512]{3,0,2,1:T(8,128)S(1)} fusion(f32[8,3,32,512]{3,0,2,1:T(8,128)S(1)} %fusion.21, f32[8,3,32,512]{3,0,2,1:T(8,128)S(1)} %get-tuple-element.43, f32[8,1,32,512]{3,0,2,1:T(8,128)S(1)} %collective-permute-done.5, f32[8,1,32,512]{3,0,2,1:T(8,128)S(1)} %collective-permute-done.4, f32[8,3,1,512]{3,0,2,1:T(8,128)S(1)} %get-tuple-element.13, ...), kind=kOutput, calls=%fused_computation.29 | output fusion | flops 9879559 | bytes 12058624 | tf_op jit(solution)/shard_map/sub | solution.py:47
  122.1 0.9 fusion.155
  122.9 5.1 %fusion.62 = f32[2,3,32,512]{3,2,1,0:T(8,128)S(1)} fusion(f32[2,3,32,512]{3,0,2,1:T(2,128)S(1)} %fusion.155), kind=kOutput, calls=%fused_computation.86 | convolution fusion | flops 607649792 | bytes 786432 | tf_op jit(solution)/shard_map/dot_general | solution.py:52
  128.1 5.1 %convolution_negate_fusion = f32[2,3,32,512]{3,2,1,0:T(8,128)S(1)} fusion(f32[2,3,32,512]{3,0,2,1:T(2,128)S(1)} %fusion.155), kind=kOutput, calls=%fused_computation.76 | convolution fusion | flops 607748096 | bytes 786432 | tf_op jit(solution)/shard_map/dot_general | solution.py:53
  134.4 0.6 fusion.52
  136.7 20.3 %copy.46 = f32[4,3,16384]{0,1,2:T(4,128)} copy(f32[4,3,16384]{2,0,1:T(4,128)S(1)} %pad_maximum_fusion.6) | data formatting | bytes 1572864 | tf_op jit(solution)/shard_map/concatenate | solution.py:120
  157.0 24.8 %reshape.88 = f32[16,1,12288]{2,1,0:T(1,128)} reshape(f32[16384,3,4]{2,1,0:T(4,128)} %bitcast.118) | data formatting | bytes 1572864
  181.8 7.3 %all-to-all-start = ((f32[16,1,12288]{2,1,0:T(1,128)}), f32[16,1,12288]{2,1,0:T(1,128)S(1)}, u32[]{:S(2)}, u32[]{:S(2)}) async-start(f32[16,1,12288]{2,1,0:T(1,128)} %reshape.88), calls=%async_computation | async-start | bytes 1572864 | tf_op jit(solution)/shard_map/all_to_all | solution.py:121
  189.3 19.3 %all-to-all-done = f32[16,1,12288]{2,1,0:T(1,128)S(1)} async-done(((f32[16,1,12288]{2,1,0:T(1,128)}), f32[16,1,12288]{2,1,0:T(1,128)S(1)}, u32[]{:S(2)}, u32[]{:S(2)}) %all-to-all-start) | async-done | bytes 786464 | tf_op jit(solution)/shard_map/all_to_all | solution.py:121
  209.1 2.5 reduce
  211.6 33.0 %reshape.89 = f32[16384,3,4]{2,1,0:T(4,128)} reshape(f32[16,12288]{1,0:T(8,128)S(1)} %reduce) | data formatting | bytes 1572864
  244.7 18.5 %copy.81 = f32[4,3,16,1024]{3,2,0,1:T(8,128)S(1)} copy(f32[4,3,16,1024]{0,1,3,2:T(4,128)} %bitcast.119) | data formatting | bytes 1572864 | tf_op jit(solution)/shard_map/all_to_all | solution.py:121
  263.6 0.7 fusion.76
  264.6 0.7 fusion.80
  265.2 0.7 fusion.49
  265.9 0.7 fusion.55
  267.9 1.4 copy.58
  269.3 4.6 %all-to-all-start.1 = ((f32[4,48,1024]{2,0,1:T(4,128)}), f32[4,48,1024]{2,0,1:T(4,128)S(1)}, u32[]{:S(2)}, u32[]{:S(2)}) async-start(f32[4,48,1024]{2,0,1:T(4,128)} %copy.58), calls=%async_computation.1 | async-start | bytes 1572864 | tf_op jit(solution)/shard_map/all_to_all | solution.py:123
  273.9 2.1 copy.61
  276.0 17.5 %all-to-all-done.1 = f32[4,48,1024]{2,0,1:T(4,128)S(1)} async-done(((f32[4,48,1024]{2,0,1:T(4,128)}), f32[4,48,1024]{2,0,1:T(4,128)S(1)}, u32[]{:S(2)}, u32[]{:S(2)}) %all-to-all-start.1) | async-done | bytes 786464 | tf_op jit(solution)/shard_map/all_to_all | solution.py:123
  296.4 5.1 %fusion.60 = f32[2,3,32,512]{3,2,1,0:T(8,128)S(1)} fusion(f32[2,3,32,512]{3,2,1,0:T(8,128)S(1)} %fusion.48), kind=kOutput, calls=%fused_computation.84 | convolution fusion | flops 607649792 | bytes 786432 | tf_op jit(solution)/shard_map/dot_general | solution.py:95
  301.5 5.6 %fusion.56 = f32[2,3,32,512]{3,2,1,0:T(8,128)} fusion(f32[2,3,32,512]{3,2,1,0:T(8,128)S(1)} %fusion.60, f32[2,3,32,512]{3,2,1,0:T(8,128)S(1)} %fusion.47), kind=kOutput, calls=%fused_computation.80 | convolution fusion | flops 607846400 | bytes 1179648 | tf_op jit(solution)/shard_map/dot_general | solution.py:95
  (56 shorter events, 12.4 us)
Async XLA Ops:
  2.5 17.9 %collective-permute-start = (f32[8,1,32,512]{3,0,2,1:T(8,128)S(1)}, f32[8,1,32,512]{3,0,2,1:T(8,128)S(1)}, u32[]{:S(2)}, u32[]{:S(2)}) collective-permute-start(f32[8,1,32,512]{3,0,2,1:T(8,128)S(1)} %get-tuple-element.36), channel_id=1, source_target_pairs={{1,0},{2,1},{3,2},{4,3},{5,4},{6,5},{7,6},{8,7},{9,8},{10,9},{11,1... | collective-permute-start | bytes 1572872 | tf_op jit(solution)/shard_map/ppermute | solution.py:19
  3.2 1.8 copy-start
  3.2 1.8 copy-start.1
  3.3 17.2 %collective-permute-start.1 = (f32[8,1,32,512]{3,0,2,1:T(8,128)S(1)}, f32[8,1,32,512]{3,0,2,1:T(8,128)S(1)}, u32[]{:S(2)}, u32[]{:S(2)}) collective-permute-start(f32[8,1,32,512]{3,0,2,1:T(8,128)S(1)} %get-tuple-element.37), channel_id=1, source_target_pairs={{0,1},{1,2},{2,3},{3,4},{4,5},{5,6},{6,7},{7,8},{8,9},{9,10},{10,1... | collective-permute-start | bytes 1572872 | tf_op jit(solution)/shard_map/ppermute | solution.py:18
  19.9 0.7 copy-start.2
  23.5 14.3 %collective-permute-start.2 = (f32[8,1,32,512]{3,0,2,1:T(8,128)S(1)}, f32[8,1,32,512]{3,0,2,1:T(8,128)S(1)}, u32[]{:S(2)}, u32[]{:S(2)}) collective-permute-start(f32[8,1,32,512]{3,0,2,1:T(8,128)S(1)} %get-tuple-element.26), channel_id=1, source_target_pairs={{1,0},{2,1},{3,2},{4,3},{5,4},{6,5},{7,6},{8,7},{9,8},{10,9},{11,1... | collective-permute-start | bytes 1572872 | tf_op jit(solution)/shard_map/ppermute | solution.py:19
  23.7 14.1 %collective-permute-start.3 = (f32[8,1,32,512]{3,0,2,1:T(8,128)S(1)}, f32[8,1,32,512]{3,0,2,1:T(8,128)S(1)}, u32[]{:S(2)}, u32[]{:S(2)}) collective-permute-start(f32[8,1,32,512]{3,0,2,1:T(8,128)S(1)} %get-tuple-element.27), channel_id=1, source_target_pairs={{0,1},{1,2},{2,3},{3,4},{4,5},{5,6},{6,7},{7,8},{8,9},{9,10},{10,1... | collective-permute-start | bytes 1572872 | tf_op jit(solution)/shard_map/ppermute | solution.py:18
  73.1 14.3 %collective-permute-start.4 = (f32[8,1,32,512]{3,0,2,1:T(8,128)S(1)}, f32[8,1,32,512]{3,0,2,1:T(8,128)S(1)}, u32[]{:S(2)}, u32[]{:S(2)}) collective-permute-start(f32[8,1,32,512]{3,0,2,1:T(8,128)S(1)} %get-tuple-element.16), channel_id=1, source_target_pairs={{1,0},{2,1},{3,2},{4,3},{5,4},{6,5},{7,6},{8,7},{9,8},{10,9},{11,1... | collective-permute-start | bytes 1572872 | tf_op jit(solution)/shard_map/ppermute | solution.py:19
  73.2 14.2 %collective-permute-start.5 = (f32[8,1,32,512]{3,0,2,1:T(8,128)S(1)}, f32[8,1,32,512]{3,0,2,1:T(8,128)S(1)}, u32[]{:S(2)}, u32[]{:S(2)}) collective-permute-start(f32[8,1,32,512]{3,0,2,1:T(8,128)S(1)} %get-tuple-element.17), channel_id=1, source_target_pairs={{0,1},{1,2},{2,3},{3,4},{4,5},{5,6},{6,7},{7,8},{8,9},{9,10},{10,1... | collective-permute-start | bytes 1572872 | tf_op jit(solution)/shard_map/ppermute | solution.py:18
  87.4 34.7 %copy-start.3 = (s32[2]{0:T(128)S(1)}, s32[2]{0:T(128)}, u32[]{:S(2)}) copy-start(s32[2]{0:T(128)} %param.7) | copy-start | bytes 28
  181.8 26.8 %all-to-all-start = ((f32[16,1,12288]{2,1,0:T(1,128)}), f32[16,1,12288]{2,1,0:T(1,128)S(1)}, u32[]{:S(2)}, u32[]{:S(2)}) async-start(f32[16,1,12288]{2,1,0:T(1,128)} %reshape.88), calls=%async_computation | async-start | bytes 1572864 | tf_op jit(solution)/shard_map/all_to_all | solution.py:121
  269.3 24.2 %all-to-all-start.1 = ((f32[4,48,1024]{2,0,1:T(4,128)}), f32[4,48,1024]{2,0,1:T(4,128)S(1)}, u32[]{:S(2)}, u32[]{:S(2)}) async-start(f32[4,48,1024]{2,0,1:T(4,128)} %copy.58), calls=%async_computation.1 | async-start | bytes 1572864 | tf_op jit(solution)/shard_map/all_to_all | solution.py:123
where the time goes:
time: 313 us; the launch traced here: 307 us
  local copies, waits for them, and re-layouts  107 us (34%)
  other arithmetic  88.9 us (28%)
  waiting for transfers between devices  60.1 us (19%)
  matrix products  32.5 us (10%)
  starting transfers between devices  18 us (6%)
    sub x3, other arithmetic, advance(): total[None] - center * center  84 us
    unnamed x11, local copies, waits for them, and re-layouts  60 us
    ppermute x3, waiting for transfers between devices, with_halo(): after = lax.ppermute(initial, axis, down)  23.3 us
    concatenate x1, local copies, waits for them, and re-layouts, shards(): stacked = jnp.concatenate([real_part, imag_part], axis=0)  20.3 us
    all_to_all x1, waiting for transfers between devices, shards(): lax.all_to_all(stacked, 'gx', split_axis=2, concat_axis=1, tiled=True)  19.3 us
    all_to_all x2, local copies, waits for them, and re-layouts, shards(): lax.all_to_all(stacked, 'gx', split_axis=2, concat_axis=1, tiled=True)  19 us
    all_to_all x1, waiting for transfers between devices, shards(): lax.all_to_all(jnp.concatenate([back_real, back_imag], axis=0), 'gx', spl...  17.5 us
    all_to_all x1, starting transfers between devices, shards(): lax.all_to_all(stacked, 'gx', split_axis=2, concat_axis=1, tiled=True)  7.34 us
  transfers between devices with their start and end apart: 8, of which 4 were waited for; matrix products, arithmetic and copies ran while one was open for 6% of the time, Pallas kernels for 0%

commit v1 on v0

--- a/solution.py
+++ b/solution.py
@@ -6,6 +6,13 @@
 
 STEPS = 3
 HIGH = lax.Precision.HIGHEST
+
+
+def divide_sector(values):
+    k_now = jnp.concatenate(
+        lax.all_to_all(jnp.stack(jnp.split(values, lax.axis_size("gx"), 2), 0), "gx", 0, 0), 1
+    )
+    return k_now
 
 
 def with_halo(value, sides, width):
@@ -118,7 +125,7 @@
     offset = lax.axis_index("gx") * columns
     real_part, imag_part = forward_planes(fields, cos_y, sin_y, cos_z, sin_z)
     stacked = jnp.concatenate([real_part, imag_part], axis=0)
-    lines = lax.all_to_all(stacked, "gx", split_axis=2, concat_axis=1, tiled=True)
+    lines = divide_sector(stacked)
     back_real, back_imag = line_power(lines[:2], lines[2:], cos_x, sin_x, offset)
     returned = lax.all_to_all(
         jnp.concatenate([back_real, back_imag], axis=0),

time: 313 us -> 218 us (0.70); the launches traced: 307 us -> 217 us
  local copies, waits for them, and re-layouts: 107 us -> 10 us
  other arithmetic: 88.9 us -> 96.2 us
    unnamed x11 -> x9, local copies, waits for them, and re-layouts: 60 us -> 3.19 us
    concatenate x1 -> x0, local copies, waits for them, and re-layouts: 20.3 us -> none  [shards(): stacked = jnp.concatenate([real_part, imag_part], axis=0)]
    all_to_all x2 -> x0, local copies, waits for them, and re-layouts: 19 us -> none  [shards(): lax.all_to_all(stacked, 'gx', split_axis=2, concat_axis=1, tiled=True)]
    unnamed x0 -> x15, other arithmetic: none -> 9.66 us
  transfers between devices with their start and end apart: 8 -> 8, of which waited for: 4 -> 4; matrix products, arithmetic and copies ran while one was open for 6% -> 9% of each run, Pallas kernels for 0% -> 0%
where the time goes in v1:
time: 218 us; the launch traced here: 217 us
  other arithmetic  96.2 us (44%)
  waiting for transfers between devices  60.5 us (28%)
  matrix products  32.5 us (15%)
  starting transfers between devices  17.2 us (8%)
  local copies, waits for them, and re-layouts  10 us (5%)
    sub x3, other arithmetic, advance(): total[None] - center * center  83.9 us
    ppermute x3, waiting for transfers between devices, with_halo(): after = lax.ppermute(initial, axis, down)  23.5 us
    all_to_all x1, waiting for transfers between devices, divide_sector(): lax.all_to_all(jnp.stack(jnp.split(values, lax.axis_size('gx'), 2), 0), '...  19.4 us
    all_to_all x1, waiting for transfers between devices, shards(): lax.all_to_all(jnp.concatenate([back_real, back_imag], axis=0), 'gx', spl...  17.5 us
    unnamed x15, other arithmetic  9.66 us
    all_to_all x1, starting transfers between devices, divide_sector(): lax.all_to_all(jnp.stack(jnp.split(values, lax.axis_size('gx'), 2), 0), '...  6.8 us
    dot_general x1, matrix products, inverse_planes(): jnp.dot(imag_z, sin_y, precision=HIGH)  5.6 us
    dot_general x1, matrix products, forward_planes(): real_y = jnp.dot(fields, cos_y, precision=HIGH)  5.12 us
  transfers between devices with their start and end apart: 8, of which 4 were waited for; matrix products, arithmetic and copies ran while one was open for 9% of the time, Pallas kernels for 0%

profile of v1, /device:TPU:11, one launch (start us, length us, event | category | flops | bytes accessed | tf_op | source)
XLA Modules:
  0.0 217.4 jit_solution(7832977143620745758)
XLA Ops:
  0.6 1.8 convert_add_fusion
  2.5 0.7 collective-permute-start
  3.2 1.2 collective-permute-start.1
  5.1 0.7 copy-done
  6.1 14.6 %multiply_subtract_fusion.2 = f32[8,3,32,512]{3,0,2,1:T(8,128)S(1)} fusion(bf16[8,3,32,512]{3,2,1,0:T(8,128)(2,1)S(1)} %copy-done.1, s32[3,32,512]{2,1,0:T(8,128)S(1)} %copy-done), kind=kOutput, calls=%fused_computation.42 | output fusion | flops 4374535 | bytes 2555904 | tf_op jit(solution)/shard_map/sub | solution.py:54
  21.5 2.2 %fusion.16 = (f32[8,3,32,512]{3,0,2,1:T(8,128)S(1)}, f32[8,3,32,512]{3,0,2,1:T(8,128)S(1)}) fusion(f32[8,3,32,512]{3,0,2,1:T(8,128)S(1)} %convert_add_fusion, f32[8,1,32,512]{3,0,2,1:T(8,128)S(1)} %collective-permute-done.1, f32[8,1,32,512]{3,0,2,1:T(8,128)S(1)} %collective-permute-done, f32[8,3,1,512]{3,0,2,1:T(8,128)S(1)} %get-tuple-element.33, ...), kind=kOutput, calls=%fused_computation.49 | convolution fusion | flops 47579328 | bytes 13828352 | tf_op jit(solution)/shard_map/gi,gxzy->ixzy/dot_general | solution.py:44
  24.4 1.7 collective-permute-start.3
  26.8 11.9 %collective-permute-done.2 = f32[8,1,32,512]{3,0,2,1:T(8,128)S(1)} collective-permute-done((f32[8,1,32,512]{3,0,2,1:T(8,128)S(1)}, f32[8,1,32,512]{3,0,2,1:T(8,128)S(1)}, u32[]{:S(2)}, u32[]{:S(2)}) %collective-permute-start.2) | collective-permute-done | bytes 524320 | tf_op jit(solution)/shard_map/ppermute | solution.py:26
  38.7 34.6 %fusion.21 = f32[8,3,32,512]{3,0,2,1:T(8,128)S(1)} fusion(f32[8,3,32,512]{3,0,2,1:T(8,128)S(1)} %get-tuple-element.42, f32[8,3,32,512]{3,0,2,1:T(8,128)S(1)} %get-tuple-element.43, f32[8,1,32,512]{3,0,2,1:T(8,128)S(1)} %collective-permute-done.3, f32[8,1,32,512]{3,0,2,1:T(8,128)S(1)} %collective-permute-done.2, f32[8,3,1,512]{3,0,2,1:T(8,128)S(1)} %get-tuple-element.23, ...), kind=kOutput, calls=%fused_computation.54 | output fusion | flops 9879559 | bytes 12058624 | tf_op jit(solution)/shard_map/sub | solution.py:54
  74.1 2.0 collective-permute-start.5
  76.6 11.7 %collective-permute-done.4 = f32[8,1,32,512]{3,0,2,1:T(8,128)S(1)} collective-permute-done((f32[8,1,32,512]{3,0,2,1:T(8,128)S(1)}, f32[8,1,32,512]{3,0,2,1:T(8,128)S(1)}, u32[]{:S(2)}, u32[]{:S(2)}) %collective-permute-start.4) | collective-permute-done | bytes 524320 | tf_op jit(solution)/shard_map/ppermute | solution.py:26
  88.3 34.6 %fusion.26 = f32[8,3,32,512]{3,0,2,1:T(8,128)S(1)} fusion(f32[8,3,32,512]{3,0,2,1:T(8,128)S(1)} %fusion.21, f32[8,3,32,512]{3,0,2,1:T(8,128)S(1)} %get-tuple-element.43, f32[8,1,32,512]{3,0,2,1:T(8,128)S(1)} %collective-permute-done.5, f32[8,1,32,512]{3,0,2,1:T(8,128)S(1)} %collective-permute-done.4, f32[8,3,1,512]{3,0,2,1:T(8,128)S(1)} %get-tuple-element.13, ...), kind=kOutput, calls=%fused_computation.59 | output fusion | flops 9879559 | bytes 12058624 | tf_op jit(solution)/shard_map/sub | solution.py:54
  123.0 0.9 fusion.172
  123.8 5.1 %fusion.62 = f32[2,3,32,512]{3,2,1,0:T(8,128)S(1)} fusion(f32[2,3,32,512]{3,0,2,1:T(2,128)S(1)} %fusion.172), kind=kOutput, calls=%fused_computation.116 | convolution fusion | flops 607649792 | bytes 786432 | tf_op jit(solution)/shard_map/dot_general | solution.py:59
  129.0 5.1 %convolution_negate_fusion = f32[2,3,32,512]{3,2,1,0:T(8,128)S(1)} fusion(f32[2,3,32,512]{3,0,2,1:T(2,128)S(1)} %fusion.172), kind=kOutput, calls=%fused_computation.106 | convolution fusion | flops 607748096 | bytes 786432 | tf_op jit(solution)/shard_map/dot_general | solution.py:60
  137.2 0.6 bitcast_dynamic-update-slice_fusion.14
  137.9 0.6 bitcast_dynamic-update-slice_fusion.13
  138.5 0.6 bitcast_dynamic-update-slice_fusion.12
  139.2 0.6 bitcast_dynamic-update-slice_fusion.11
  139.8 0.6 bitcast_dynamic-update-slice_fusion.10
  147.5 6.8 %all-to-all-start = ((f32[16,4,3,1024]{3,1,2,0:T(4,128)}), f32[16,4,3,1024]{3,1,2,0:T(4,128)S(1)}, u32[]{:S(2)}, u32[]{:S(2)}) async-start(f32[16,4,3,1024]{3,1,2,0:T(4,128)} %fusion.100), calls=%async_computation | async-start | bytes 1572864 | tf_op jit(solution)/shard_map/all_to_all | solution.py:13
  154.5 19.4 %all-to-all-done = f32[16,4,3,1024]{3,1,2,0:T(4,128)S(1)} async-done(((f32[16,4,3,1024]{3,1,2,0:T(4,128)}), f32[16,4,3,1024]{3,1,2,0:T(4,128)S(1)}, u32[]{:S(2)}, u32[]{:S(2)}) %all-to-all-start) | async-done | bytes 786464 | tf_op jit(solution)/shard_map/all_to_all | solution.py:13
  174.2 0.7 fusion.76
  174.9 0.7 fusion.80
  175.6 0.7 fusion.49
  176.2 0.7 fusion.55
  178.2 1.4 copy.53
  179.6 4.6 %all-to-all-start.1 = ((f32[4,48,1024]{2,0,1:T(4,128)}), f32[4,48,1024]{2,0,1:T(4,128)S(1)}, u32[]{:S(2)}, u32[]{:S(2)}) async-start(f32[4,48,1024]{2,0,1:T(4,128)} %copy.53), calls=%async_computation.1 | async-start | bytes 1572864 | tf_op jit(solution)/shard_map/all_to_all | solution.py:130
  184.3 2.1 copy.56
  186.3 17.5 %all-to-all-done.1 = f32[4,48,1024]{2,0,1:T(4,128)S(1)} async-done(((f32[4,48,1024]{2,0,1:T(4,128)}), f32[4,48,1024]{2,0,1:T(4,128)S(1)}, u32[]{:S(2)}, u32[]{:S(2)}) %all-to-all-start.1) | async-done | bytes 786464 | tf_op jit(solution)/shard_map/all_to_all | solution.py:130
  206.8 5.1 %fusion.60 = f32[2,3,32,512]{3,2,1,0:T(8,128)S(1)} fusion(f32[2,3,32,512]{3,2,1,0:T(8,128)S(1)} %fusion.48), kind=kOutput, calls=%fused_computation.114 | convolution fusion | flops 607649792 | bytes 786432 | tf_op jit(solution)/shard_map/dot_general | solution.py:102
  211.9 5.6 %fusion.56 = f32[2,3,32,512]{3,2,1,0:T(8,128)} fusion(f32[2,3,32,512]{3,2,1,0:T(8,128)S(1)} %fusion.60, f32[2,3,32,512]{3,2,1,0:T(8,128)S(1)} %fusion.47), kind=kOutput, calls=%fused_computation.110 | convolution fusion | flops 607846400 | bytes 1179648 | tf_op jit(solution)/shard_map/dot_general | solution.py:102
  (63 shorter events, 19.0 us)
Async XLA Ops:
  2.5 18.8 %collective-permute-start = (f32[8,1,32,512]{3,0,2,1:T(8,128)S(1)}, f32[8,1,32,512]{3,0,2,1:T(8,128)S(1)}, u32[]{:S(2)}, u32[]{:S(2)}) collective-permute-start(f32[8,1,32,512]{3,0,2,1:T(8,128)S(1)} %get-tuple-element.36), channel_id=1, source_target_pairs={{1,0},{2,1},{3,2},{4,3},{5,4},{6,5},{7,6},{8,7},{9,8},{10,9},{11,1... | collective-permute-start | bytes 1572872 | tf_op jit(solution)/shard_map/ppermute | solution.py:26
  3.2 18.1 %collective-permute-start.1 = (f32[8,1,32,512]{3,0,2,1:T(8,128)S(1)}, f32[8,1,32,512]{3,0,2,1:T(8,128)S(1)}, u32[]{:S(2)}, u32[]{:S(2)}) collective-permute-start(f32[8,1,32,512]{3,0,2,1:T(8,128)S(1)} %get-tuple-element.37), channel_id=1, source_target_pairs={{0,1},{1,2},{2,3},{3,4},{4,5},{5,6},{6,7},{7,8},{8,9},{9,10},{10,1... | collective-permute-start | bytes 1572872 | tf_op jit(solution)/shard_map/ppermute | solution.py:25
  4.9 0.9 copy-start
  4.9 1.2 copy-start.1
  20.8 0.7 copy-start.2
  24.4 14.3 %collective-permute-start.2 = (f32[8,1,32,512]{3,0,2,1:T(8,128)S(1)}, f32[8,1,32,512]{3,0,2,1:T(8,128)S(1)}, u32[]{:S(2)}, u32[]{:S(2)}) collective-permute-start(f32[8,1,32,512]{3,0,2,1:T(8,128)S(1)} %get-tuple-element.26), channel_id=1, source_target_pairs={{1,0},{2,1},{3,2},{4,3},{5,4},{6,5},{7,6},{8,7},{9,8},{10,9},{11,1... | collective-permute-start | bytes 1572872 | tf_op jit(solution)/shard_map/ppermute | solution.py:26
  24.4 14.2 %collective-permute-start.3 = (f32[8,1,32,512]{3,0,2,1:T(8,128)S(1)}, f32[8,1,32,512]{3,0,2,1:T(8,128)S(1)}, u32[]{:S(2)}, u32[]{:S(2)}) collective-permute-start(f32[8,1,32,512]{3,0,2,1:T(8,128)S(1)} %get-tuple-element.27), channel_id=1, source_target_pairs={{0,1},{1,2},{2,3},{3,4},{4,5},{5,6},{6,7},{7,8},{8,9},{9,10},{10,1... | collective-permute-start | bytes 1572872 | tf_op jit(solution)/shard_map/ppermute | solution.py:25
  74.0 14.3 %collective-permute-start.4 = (f32[8,1,32,512]{3,0,2,1:T(8,128)S(1)}, f32[8,1,32,512]{3,0,2,1:T(8,128)S(1)}, u32[]{:S(2)}, u32[]{:S(2)}) collective-permute-start(f32[8,1,32,512]{3,0,2,1:T(8,128)S(1)} %get-tuple-element.16), channel_id=1, source_target_pairs={{1,0},{2,1},{3,2},{4,3},{5,4},{6,5},{7,6},{8,7},{9,8},{10,9},{11,1... | collective-permute-start | bytes 1572872 | tf_op jit(solution)/shard_map/ppermute | solution.py:26
  74.1 14.2 %collective-permute-start.5 = (f32[8,1,32,512]{3,0,2,1:T(8,128)S(1)}, f32[8,1,32,512]{3,0,2,1:T(8,128)S(1)}, u32[]{:S(2)}, u32[]{:S(2)}) collective-permute-start(f32[8,1,32,512]{3,0,2,1:T(8,128)S(1)} %get-tuple-element.17), channel_id=1, source_target_pairs={{0,1},{1,2},{2,3},{3,4},{4,5},{5,6},{6,7},{7,8},{8,9},{9,10},{10,1... | collective-permute-start | bytes 1572872 | tf_op jit(solution)/shard_map/ppermute | solution.py:25
  88.3 34.7 %copy-start.3 = (s32[2]{0:T(128)S(1)}, s32[2]{0:T(128)}, u32[]{:S(2)}) copy-start(s32[2]{0:T(128)} %param.7) | copy-start | bytes 28
  147.5 26.4 %all-to-all-start = ((f32[16,4,3,1024]{3,1,2,0:T(4,128)}), f32[16,4,3,1024]{3,1,2,0:T(4,128)S(1)}, u32[]{:S(2)}, u32[]{:S(2)}) async-start(f32[16,4,3,1024]{3,1,2,0:T(4,128)} %fusion.100), calls=%async_computation | async-start | bytes 1572864 | tf_op jit(solution)/shard_map/all_to_all | solution.py:13
  179.6 24.2 %all-to-all-start.1 = ((f32[4,48,1024]{2,0,1:T(4,128)}), f32[4,48,1024]{2,0,1:T(4,128)S(1)}, u32[]{:S(2)}, u32[]{:S(2)}) async-start(f32[4,48,1024]{2,0,1:T(4,128)} %copy.53), calls=%async_computation.1 | async-start | bytes 1572864 | tf_op jit(solution)/shard_map/all_to_all | solution.py:130
